TPU v7x, 256 devices: a whole 4x4x8 slice. The times are simulated.
256 devices in a mesh: row: 16 (over y, z_lo), col: 16 (over z_hi, x, core).
Axes of the slice: x: 4, y: 4, z: 8 (z_hi: 2, z_lo: 4; z = z_hi * 4 + z_lo), core: 2. Of those that a mesh axis runs over, the one named last changes fastest.
Arguments:
- start_vectors: float32 [64, 32768], P(None, ('row', 'col')), may hold values from -6 to 6
- cluster_order: int32 [256, 128], P(('row', 'col')), may hold values from 0 to 127, each once within a row
- weights: bfloat16 [32768, 16, 2048], P('row', 'col'), may hold values from 0 to 1, as said below
- block_mask: int32 [256, 16, 16], P('row', 'col'), may hold values 0 or 1
Outputs:
- embedding: float32 [64, 32768], P(None, ('row', 'col'))
Inputs may be any that keep to these rules, and one draw needn't show every extreme that they name: Each row of cluster_order holds every number of 0 to 127 once. `block_mask`: entries below the diagonal blocks are read only through their mirror. `weights`: every node except the last of its cluster block has a positive weight to the next node of its cluster block.
All inputs are finite; a program needn't handle non-finite values.
Results may differ from a plain program's by a relative error of at most 0.00087.
Values may be sent and summed in bfloat16 or wider, within the bound.
A program may use at most 64 MiB of HBM per device.

v0:
```python
import math
import jax
import jax.numpy as jnp
from jax import lax
from jax.sharding import PartitionSpec as P

ITERS = 3


def orthonormalize(panel_in):
    partial_gram = lax.dot_general(
        panel_in,
        panel_in,
        (((1,), (1,)), ((), ())),
        precision=lax.Precision.HIGHEST,
        preferred_element_type=jnp.float32,
    )
    total_gram = lax.psum(partial_gram, ("row", "col"))
    factor = jnp.linalg.cholesky(total_gram)
    return jax.scipy.linalg.solve_triangular(factor, panel_in, lower=True)


def collect_direct(term):
    return lax.psum_scatter(term, "col", scatter_dimension=1, tiled=True)


def direct_part(matrix, vectors):
    return lax.dot_general(
        lax.all_gather(vectors, "row", axis=1, tiled=True),
        matrix,
        (((1,), (1,)), ((), ())),
        preferred_element_type=jnp.float32,
    )


def local(start_vectors, cluster_order, weights, block_mask):
    row_index = lax.axis_index("row")
    col_index = lax.axis_index("col")
    row_count = lax.axis_size("row")
    col_count = lax.axis_size("col")
    block_len = start_vectors.shape[1]
    stored = weights[:, 0, :]
    live_mask = block_mask[:, 0, :]
    local_rows = row_index * col_count * block_len + jnp.arange(
        col_count * block_len, dtype=jnp.int32
    )
    col_position = jnp.arange(row_count * block_len, dtype=jnp.int32)
    local_cols = (
        col_position // block_len * col_count + col_index
    ) * block_len + col_position % block_len
    row_spans = row_index * col_count + jnp.arange(col_count, dtype=jnp.int32)
    col_spans = jnp.arange(row_count, dtype=jnp.int32) * col_count + col_index
    same_block = row_spans[:, None] == col_spans[None, :]
    keep_upper = ((live_mask > 0) | same_block)[:, None, :, None] & (
        local_rows.reshape(col_count, block_len, 1, 1)
        < local_cols.reshape(1, 1, row_count, block_len)
    )
    zero_value = jnp.zeros((), jnp.bfloat16)
    upper_part = jnp.where(
        keep_upper, stored.reshape(col_count, block_len, row_count, block_len), zero_value
    )
    ones_cols = jnp.ones((row_count * block_len,), jnp.bfloat16)
    matrix = upper_part.reshape(col_count * block_len, row_count * block_len)
    ones_rows = jnp.ones((col_count * block_len,), jnp.bfloat16)

    def mirror_sums(term):
        return lax.psum_scatter(term, "row", scatter_dimension=1, tiled=True)

    row_totals = jnp.dot(matrix, ones_cols, preferred_element_type=jnp.float32)[None, :]
    col_totals = jnp.dot(ones_rows, matrix, preferred_element_type=jnp.float32)[None, :]
    degree = collect_direct(row_totals) + mirror_sums(col_totals)
    inverse_root = 1.0 / jnp.sqrt(degree)
    picked = jnp.take_along_axis(
        start_vectors, jnp.broadcast_to(cluster_order, start_vectors.shape), axis=1
    )
    panel_now = orthonormalize(picked)
    for round_index in range(ITERS):
        vectors = (inverse_root * panel_now).astype(jnp.bfloat16)
        panel_now = orthonormalize(
            panel_now
            + inverse_root
            * (
                collect_direct(direct_part(matrix, vectors))
                + mirror_sums(
                    jnp.dot(
                        lax.all_gather(vectors, "col", axis=1, tiled=True),
                        matrix,
                        preferred_element_type=jnp.float32,
                    )
                )
            )
        )
    total_nodes = block_len * row_count * col_count
    return math.sqrt(total_nodes) * panel_now


def solution(mesh):
    placed = (
        P(None, ("row", "col")),
        P(("row", "col"), None),
        P("row", "col", None),
        P("row", "col", None),
    )
    return jax.shard_map(
        local, mesh=mesh, in_specs=placed, out_specs=P(None, ("row", "col")), check_vma=False
    )
```

profile of v0, /device:TPU:1, one launch (start us, length us, event | category | flops | bytes accessed | tf_op | source)
XLA Modules:
  0.0 1080.2 jit_solution(14854760492870772984)
XLA Ops:
  6.5 0.7 broadcast_compare_fusion
  7.4 1.1 and.66
  8.5 7.7 fusion
  16.3 3.2 copy-done.1
  19.5 3.4 convolution_bitcast_fusion.1
  23.0 7.7 convolution_bitcast_fusion
  30.9 50.7 %gather_fusion = f32[8192]{0:T(1024)S(1)} fusion(f32[64,128]{1,0:T(8,128)S(1)} %copy-done, s32[8192]{0:T(1024)S(1)} %or_bitcast_fusion), kind=kCustom, calls=%fused_computation | custom fusion | bytes 131072 | tf_op jit(solution)/shard_map/jit(take_along_axis)/gather | solution.py:73
  81.7 82.8 %psum.28 = f32[64,64]{0,1:T(8,128)S(1)} all-reduce(f32[64,64]{0,1:T(8,128)S(1)} %fusion.16), channel_id=1, replica_groups=mesh['row'=16,'col'=16] {'row','col'}, use_global_device_ids=true, to_apply=%region_0.1 | all-reduce | flops 4096 | bytes 32768 | tf_op jit(solution)/shard_map/psum | solution.py:18
  164.7 5.8 cholesky.74
  171.2 0.7 fusion.1
  171.8 4.9 custom-call.10
  176.8 0.9 copy.34
  177.7 4.9 reduce-scatter.27.cloned.1.call-done
  182.5 0.9 copy.36
  183.7 32.5 %all_gather.18 = bf16[64,2048]{1,0:T(8,128)(2,1)S(1)} all-gather(bf16[64,128]{1,0:T(8,128)(2,1)S(1)} %get-tuple-element.6), channel_id=1, replica_groups=mesh['row'=16,'col'=16] {'row'}, dimensions={1}, use_global_device_ids=true | all-gather | bytes 278528 | tf_op jit(solution)/shard_map/all_gather | solution.py:29
  216.2 6.9 fusion.59
  223.1 50.3 %all_gather.19 = bf16[64,2048]{1,0:T(8,128)(2,1)S(1)} all-gather(bf16[64,128]{1,0:T(8,128)(2,1)S(1)} %get-tuple-element.6), channel_id=1, replica_groups=mesh['row'=16,'col'=16] {'col'}, dimensions={1}, use_global_device_ids=true | all-gather | bytes 278528 | tf_op jit(solution)/shard_map/all_gather | solution.py:86
  273.5 5.8 fusion.60
  279.4 35.2 %reduce-scatter.13.cloned.1.call-done = f32[64,128]{1,0:T(8,128)} async-done(((f32[64,2048]{1,0:T(8,128)}), f32[64,128]{1,0:T(8,128)}) %reduce-scatter.13.cloned.1.call-update) | async-done | bytes 32784 | tf_op jit(solution)/shard_map/reduce_scatter | solution.py:24
  314.6 75.0 %reduce-scatter.15.cloned.1.call-done = f32[64,128]{1,0:T(8,128)} async-done(((f32[64,2048]{1,0:T(8,128)}), f32[64,128]{1,0:T(8,128)}) %reduce-scatter.15.cloned.1.call-update) | async-done | bytes 32784 | tf_op jit(solution)/shard_map/reduce_scatter | solution.py:67
  389.6 0.8 multiply_add_fusion.2
  390.6 85.2 %psum.29 = f32[64,64]{0,1:T(8,128)S(1)} all-reduce(f32[64,64]{0,1:T(8,128)S(1)} %fusion.61), channel_id=1, replica_groups=mesh['row'=16,'col'=16] {'row','col'}, use_global_device_ids=true, to_apply=%region_7.10 | all-reduce | flops 4096 | bytes 32768 | tf_op jit(solution)/shard_map/psum | solution.py:18
  475.8 5.8 cholesky.85
  482.3 0.7 fusion.2
  483.0 4.9 custom-call.11
  488.2 34.1 %all_gather.20 = bf16[64,2048]{1,0:T(8,128)(2,1)S(1)} all-gather(bf16[64,128]{1,0:T(8,128)(2,1)S(1)} %get-tuple-element.9), channel_id=1, replica_groups=mesh['row'=16,'col'=16] {'row'}, dimensions={1}, use_global_device_ids=true | all-gather | bytes 278528 | tf_op jit(solution)/shard_map/all_gather | solution.py:29
  522.3 6.9 fusion.62
  529.2 36.1 %all_gather.21 = bf16[64,2048]{1,0:T(8,128)(2,1)S(1)} all-gather(bf16[64,128]{1,0:T(8,128)(2,1)S(1)} %get-tuple-element.9), channel_id=1, replica_groups=mesh['row'=16,'col'=16] {'col'}, dimensions={1}, use_global_device_ids=true | all-gather | bytes 278528 | tf_op jit(solution)/shard_map/all_gather | solution.py:86
  565.3 5.8 fusion.63
  571.2 35.5 %reduce-scatter.17.cloned.1.call-done = f32[64,128]{1,0:T(8,128)} async-done(((f32[64,2048]{1,0:T(8,128)}), f32[64,128]{1,0:T(8,128)}) %reduce-scatter.17.cloned.1.call-update) | async-done | bytes 32784 | tf_op jit(solution)/shard_map/reduce_scatter | solution.py:24
  606.7 74.7 %reduce-scatter.19.cloned.1.call-done = f32[64,128]{1,0:T(8,128)} async-done(((f32[64,2048]{1,0:T(8,128)}), f32[64,128]{1,0:T(8,128)}) %reduce-scatter.19.cloned.1.call-update) | async-done | bytes 32784 | tf_op jit(solution)/shard_map/reduce_scatter | solution.py:67
  681.4 0.8 multiply_add_fusion.1
  682.4 85.6 %psum.30 = f32[64,64]{0,1:T(8,128)S(1)} all-reduce(f32[64,64]{0,1:T(8,128)S(1)} %fusion.64), channel_id=1, replica_groups=mesh['row'=16,'col'=16] {'row','col'}, use_global_device_ids=true, to_apply=%region_10.13 | all-reduce | flops 4096 | bytes 32768 | tf_op jit(solution)/shard_map/psum | solution.py:18
  768.1 5.8 cholesky.96
  774.6 0.7 fusion.3
  775.3 4.9 custom-call.12
  780.4 34.1 %all_gather.22 = bf16[64,2048]{1,0:T(8,128)(2,1)S(1)} all-gather(bf16[64,128]{1,0:T(8,128)(2,1)S(1)} %get-tuple-element.11), channel_id=1, replica_groups=mesh['row'=16,'col'=16] {'row'}, dimensions={1}, use_global_device_ids=true | all-gather | bytes 278528 | tf_op jit(solution)/shard_map/all_gather | solution.py:29
  814.5 6.9 fusion.65
  821.5 35.9 %all_gather.23 = bf16[64,2048]{1,0:T(8,128)(2,1)S(1)} all-gather(bf16[64,128]{1,0:T(8,128)(2,1)S(1)} %get-tuple-element.11), channel_id=1, replica_groups=mesh['row'=16,'col'=16] {'col'}, dimensions={1}, use_global_device_ids=true | all-gather | bytes 278528 | tf_op jit(solution)/shard_map/all_gather | solution.py:86
  857.4 5.8 fusion.66
  863.2 35.7 %reduce-scatter.21.cloned.1.call-done = f32[64,128]{1,0:T(8,128)} async-done(((f32[64,2048]{1,0:T(8,128)}), f32[64,128]{1,0:T(8,128)}) %reduce-scatter.21.cloned.1.call-update) | async-done | bytes 32784 | tf_op jit(solution)/shard_map/reduce_scatter | solution.py:24
  899.0 75.8 %reduce-scatter.23.cloned.1.call-done = f32[64,128]{1,0:T(8,128)} async-done(((f32[64,2048]{1,0:T(8,128)}), f32[64,128]{1,0:T(8,128)}) %reduce-scatter.23.cloned.1.call-update) | async-done | bytes 32784 | tf_op jit(solution)/shard_map/reduce_scatter | solution.py:67
  974.7 0.8 multiply_add_fusion
  975.7 84.6 %psum.31 = f32[64,64]{0,1:T(8,128)S(1)} all-reduce(f32[64,64]{0,1:T(8,128)S(1)} %fusion.67), channel_id=1, replica_groups=mesh['row'=16,'col'=16] {'row','col'}, use_global_device_ids=true, to_apply=%region_13.16 | all-reduce | flops 4096 | bytes 32768 | tf_op jit(solution)/shard_map/psum | solution.py:18
  1060.4 5.8 cholesky.107
  1066.9 0.7 fusion.4
  1067.6 4.9 custom-call.13
  1072.5 0.9 convolution_multiply_fusion
  (52 shorter events, 5.1 us)
Async XLA Ops:
  6.5 24.3 %copy-start = (f32[64,128]{1,0:T(8,128)S(1)}, f32[64,128]{1,0:T(8,128)}, u32[]{:S(2)}) copy-start(f32[64,128]{1,0:T(8,128)} %param.7) | copy-start | bytes 98308
  6.5 170.2 %reduce-scatter.25.cloned.1.call-start = ((), (), s32[]{:S(2)}) async-start(), calls=%async_computation.14 | async-start | bytes 1114112
  16.3 3.2 copy-start.1
  22.9 7.9 copy-start.2
  22.9 159.6 %reduce-scatter.27.cloned.1.call-start = ((), (), s32[]{:S(2)}) async-start(), calls=%async_computation.15 | async-start | bytes 1114112
  30.7 283.8 %reduce-scatter.13.cloned.1.call-start = ((), (), s32[]{:S(2)}) async-start(), calls=%async_computation.8 | async-start | bytes 557056 | tf_op jit(solution)/shard_map/reduce_scatter | solution.py:24
  223.1 166.5 %reduce-scatter.15.cloned.1.call-start = ((), (), s32[]{:S(2)}) async-start(), calls=%async_computation.9 | async-start | bytes 557056 | tf_op jit(solution)/shard_map/reduce_scatter | solution.py:67
  279.3 327.4 %reduce-scatter.17.cloned.1.call-start = ((), (), s32[]{:S(2)}) async-start(), calls=%async_computation.10 | async-start | bytes 557056 | tf_op jit(solution)/shard_map/reduce_scatter | solution.py:24
  529.2 152.2 %reduce-scatter.19.cloned.1.call-start = ((), (), s32[]{:S(2)}) async-start(), calls=%async_computation.11 | async-start | bytes 557056 | tf_op jit(solution)/shard_map/reduce_scatter | solution.py:67
  571.1 327.8 %reduce-scatter.21.cloned.1.call-start = ((), (), s32[]{:S(2)}) async-start(), calls=%async_computation.12 | async-start | bytes 557056 | tf_op jit(solution)/shard_map/reduce_scatter | solution.py:24
  821.4 153.3 %reduce-scatter.23.cloned.1.call-start = ((), (), s32[]{:S(2)}) async-start(), calls=%async_computation.13 | async-start | bytes 557056 | tf_op jit(solution)/shard_map/reduce_scatter | solution.py:67
Sparse Core Ops, SparseCore 0:
  23.1 81.6 reduce-scatter.24
  107.3 75.2 reduce-scatter.26
  223.2 91.2 reduce-scatter.12
  316.9 72.6 reduce-scatter.14
  529.3 77.3 reduce-scatter.16
  609.1 72.2 reduce-scatter.18
  821.5 77.3 reduce-scatter.20
  901.4 73.2 reduce-scatter.22
where the time goes:
time: 1080 us
  blocking collectives  561 us (52%)
  waiting for transfers between devices  337 us (31%)
  other arithmetic  59.2 us (5%)
  local copies, waits for them, and re-layouts  57.1 us (5%)
  matrix products  51.7 us (5%)
  between operations  13.8 us (1%)
    psum x4, blocking collectives, orthonormalize(): total_gram = lax.psum(partial_gram, ('row', 'col'))  338 us
    reduce_scatter x3, waiting for transfers between devices, mirror_sums(): return lax.psum_scatter(term, 'row', scatter_dimension=1, tiled=True)  225 us
    all_gather x3, blocking collectives, local(): lax.all_gather(vectors, 'col', axis=1, tiled=True)  122 us
    reduce_scatter x3, waiting for transfers between devices, collect_direct(): return lax.psum_scatter(term, 'col', scatter_dimension=1, tiled=True)  106 us
    all_gather x3, blocking collectives, direct_part(): lax.all_gather(vectors, 'row', axis=1, tiled=True)  101 us
    gather x1, local copies, waits for them, and re-layouts, local(): jnp.take_along_axis(start_vectors, jnp.broadcast_to(cluster_order, start_...  50.7 us
    another operation x12, other arithmetic, orthonormalize(): factor = jnp.linalg.cholesky(total_gram)  26.1 us
    another operation x8, other arithmetic, orthonormalize(): return jax.scipy.linalg.solve_triangular(factor, panel_in, lower=True)  22.2 us
  transfers between devices with their start and end apart: 8, of which 7 were waited for; matrix products, arithmetic and copies ran while one was open for 8% of the time, Pallas kernels for 0%

commit v1 on v0

--- a/solution.py
+++ b/solution.py
@@ -15,7 +15,7 @@
         precision=lax.Precision.HIGHEST,
         preferred_element_type=jnp.float32,
     )
-    total_gram = lax.psum(partial_gram, ("row", "col"))
+    total_gram = jnp.sum(lax.all_gather(partial_gram, ("row", "col")), axis=0)
     factor = jnp.linalg.cholesky(total_gram)
     return jax.scipy.linalg.solve_triangular(factor, panel_in, lower=True)
 

time: 1080 us -> 2450 us (2.27)
  waiting for transfers between devices: 337 us -> 2030 us
  blocking collectives: 561 us -> 213 us
    all_gather x0 -> x4, waiting for transfers between devices: none -> 1600 us  [orthonormalize(): total_gram = jnp.sum(lax.all_gather(partial_gram, ('row', 'col')), axis=0)]
    psum x4 -> x0, blocking collectives: 338 us -> none  [orthonormalize(): total_gram = lax.psum(partial_gram, ('row', 'col'))]
    unnamed x10 -> x14, waiting for transfers between devices: 5.01 us -> 98.3 us
  transfers between devices with their start and end apart: 8 -> 12, of which waited for: 7 -> 12; matrix products, arithmetic and copies ran while one was open for 8% -> 3% of each run, Pallas kernels for 0% -> 0%
where the time goes in v1:
time: 2450 us
  waiting for transfers between devices  2030 us (83%)
  blocking collectives  213 us (9%)
  other arithmetic  75.2 us (3%)
  local copies, waits for them, and re-layouts  57.2 us (2%)
  matrix products  54.1 us (2%)
    all_gather x4, waiting for transfers between devices, orthonormalize(): total_gram = jnp.sum(lax.all_gather(partial_gram, ('row', 'col')), axis=0)  1600 us
    reduce_scatter x3, waiting for transfers between devices, mirror_sums(): return lax.psum_scatter(term, 'row', scatter_dimension=1, tiled=True)  225 us
    all_gather x3, blocking collectives, local(): lax.all_gather(vectors, 'col', axis=1, tiled=True)  114 us
    reduce_scatter x3, waiting for transfers between devices, collect_direct(): return lax.psum_scatter(term, 'col', scatter_dimension=1, tiled=True)  109 us
    all_gather x3, blocking collectives, direct_part(): lax.all_gather(vectors, 'row', axis=1, tiled=True)  99.4 us
    unnamed x14, waiting for transfers between devices  98.3 us
    gather x1, local copies, waits for them, and re-layouts, local(): jnp.take_along_axis(start_vectors, jnp.broadcast_to(cluster_order, start_...  50.7 us
  transfers between devices with their start and end apart: 12, of which 12 were waited for; matrix products, arithmetic and copies ran while one was open for 3% of the time, Pallas kernels for 0%

profile of v1, /device:TPU:1, one launch (start us, length us, event | category | flops | bytes accessed | tf_op | source)
XLA Modules:
  0.0 2448.8 jit_solution(16080691237863748192)
XLA Ops:
  8.2 1.1 and.66
  9.4 7.7 fusion
  17.1 3.2 copy-done.1
  20.3 3.4 convolution_bitcast_fusion.1
  23.8 7.8 convolution_bitcast_fusion
  31.7 50.7 %gather_fusion = f32[8192]{0:T(1024)S(1)} fusion(f32[64,128]{1,0:T(8,128)S(1)} %copy-done, s32[8192]{0:T(1024)S(1)} %or_bitcast_fusion), kind=kCustom, calls=%fused_computation | custom fusion | bytes 131072 | tf_op jit(solution)/shard_map/jit(take_along_axis)/gather | solution.py:73
  82.4 0.8 fusion.16
  83.4 22.1 reduce-scatter.25.cloned.1.call-done
  105.5 0.9 copy.18
  106.4 76.1 %reduce-scatter.27.cloned.1.call-done = f32[128,1]{1,0:T(8,128)} async-done(((f32[2048,1]{1,0:T(8,128)}), f32[128,1]{1,0:T(8,128)}) %reduce-scatter.27.cloned.1.call-update) | async-done | bytes 528
  182.5 0.9 copy.20
  183.4 322.2 %all-gather.9.cloned.1.call-done = f32[16384,64]{1,0:T(8,128)} async-done(((f32[64,64]{1,0:T(8,128)}), f32[16384,64]{1,0:T(8,128)}) %all-gather.9.cloned.1.call-update) | async-done | bytes 4194320 | tf_op jit(solution)/shard_map/all_gather | solution.py:18
  505.6 4.0 reduce_sum.36
  509.7 5.8 cholesky.74
  516.9 4.9 custom-call.10
  522.1 33.3 %all_gather.44 = bf16[64,2048]{1,0:T(8,128)(2,1)S(1)} all-gather(bf16[64,128]{1,0:T(8,128)(2,1)S(1)} %get-tuple-element.6), channel_id=1, replica_groups=mesh['row'=16,'col'=16] {'row'}, dimensions={1}, use_global_device_ids=true | all-gather | bytes 278528 | tf_op jit(solution)/shard_map/all_gather | solution.py:29
  555.3 6.9 fusion.59
  562.3 37.7 %all_gather.45 = bf16[64,2048]{1,0:T(8,128)(2,1)S(1)} all-gather(bf16[64,128]{1,0:T(8,128)(2,1)S(1)} %get-tuple-element.6), channel_id=1, replica_groups=mesh['row'=16,'col'=16] {'col'}, dimensions={1}, use_global_device_ids=true | all-gather | bytes 278528 | tf_op jit(solution)/shard_map/all_gather | solution.py:86
  599.9 5.8 fusion.60
  605.8 36.3 %reduce-scatter.13.cloned.1.call-done = f32[64,128]{1,0:T(8,128)} async-done(((f32[64,2048]{1,0:T(8,128)}), f32[64,128]{1,0:T(8,128)}) %reduce-scatter.13.cloned.1.call-update) | async-done | bytes 32784 | tf_op jit(solution)/shard_map/reduce_scatter | solution.py:24
  642.2 75.6 %reduce-scatter.15.cloned.1.call-done = f32[64,128]{1,0:T(8,128)} async-done(((f32[64,2048]{1,0:T(8,128)}), f32[64,128]{1,0:T(8,128)}) %reduce-scatter.15.cloned.1.call-update) | async-done | bytes 32784 | tf_op jit(solution)/shard_map/reduce_scatter | solution.py:67
  718.6 0.8 fusion.61
  719.5 425.6 %all-gather.11.cloned.1.call-done = f32[16384,64]{1,0:T(8,128)} async-done(((f32[64,64]{1,0:T(8,128)}), f32[16384,64]{1,0:T(8,128)}) %all-gather.11.cloned.1.call-update) | async-done | bytes 4194320 | tf_op jit(solution)/shard_map/all_gather | solution.py:18
  1145.1 4.0 reduce_sum.37
  1149.2 5.8 cholesky.85
  1156.4 4.9 custom-call.11
  1161.5 33.1 %all_gather.48 = bf16[64,2048]{1,0:T(8,128)(2,1)S(1)} all-gather(bf16[64,128]{1,0:T(8,128)(2,1)S(1)} %get-tuple-element.9), channel_id=1, replica_groups=mesh['row'=16,'col'=16] {'row'}, dimensions={1}, use_global_device_ids=true | all-gather | bytes 278528 | tf_op jit(solution)/shard_map/all_gather | solution.py:29
  1194.6 6.9 fusion.62
  1201.6 38.0 %all_gather.49 = bf16[64,2048]{1,0:T(8,128)(2,1)S(1)} all-gather(bf16[64,128]{1,0:T(8,128)(2,1)S(1)} %get-tuple-element.9), channel_id=1, replica_groups=mesh['row'=16,'col'=16] {'col'}, dimensions={1}, use_global_device_ids=true | all-gather | bytes 278528 | tf_op jit(solution)/shard_map/all_gather | solution.py:86
  1239.6 5.8 fusion.63
  1245.5 36.1 %reduce-scatter.17.cloned.1.call-done = f32[64,128]{1,0:T(8,128)} async-done(((f32[64,2048]{1,0:T(8,128)}), f32[64,128]{1,0:T(8,128)}) %reduce-scatter.17.cloned.1.call-update) | async-done | bytes 32784 | tf_op jit(solution)/shard_map/reduce_scatter | solution.py:24
  1281.6 74.7 %reduce-scatter.19.cloned.1.call-done = f32[64,128]{1,0:T(8,128)} async-done(((f32[64,2048]{1,0:T(8,128)}), f32[64,128]{1,0:T(8,128)}) %reduce-scatter.19.cloned.1.call-update) | async-done | bytes 32784 | tf_op jit(solution)/shard_map/reduce_scatter | solution.py:67
  1358.0 426.6 %all-gather.13.cloned.1.call-done = f32[16384,64]{1,0:T(8,128)} async-done(((f32[64,64]{1,0:T(8,128)}), f32[16384,64]{1,0:T(8,128)}) %all-gather.13.cloned.1.call-update) | async-done | bytes 4194320 | tf_op jit(solution)/shard_map/all_gather | solution.py:18
  1784.6 4.0 reduce_sum.38
  1788.7 5.8 cholesky.96
  1795.9 4.9 custom-call.12
  1801.0 33.1 %all_gather.52 = bf16[64,2048]{1,0:T(8,128)(2,1)S(1)} all-gather(bf16[64,128]{1,0:T(8,128)(2,1)S(1)} %get-tuple-element.11), channel_id=1, replica_groups=mesh['row'=16,'col'=16] {'row'}, dimensions={1}, use_global_device_ids=true | all-gather | bytes 278528 | tf_op jit(solution)/shard_map/all_gather | solution.py:29
  1834.1 6.9 fusion.65
  1841.1 37.8 %all_gather.53 = bf16[64,2048]{1,0:T(8,128)(2,1)S(1)} all-gather(bf16[64,128]{1,0:T(8,128)(2,1)S(1)} %get-tuple-element.11), channel_id=1, replica_groups=mesh['row'=16,'col'=16] {'col'}, dimensions={1}, use_global_device_ids=true | all-gather | bytes 278528 | tf_op jit(solution)/shard_map/all_gather | solution.py:86
  1878.9 5.8 fusion.66
  1884.8 36.3 %reduce-scatter.21.cloned.1.call-done = f32[64,128]{1,0:T(8,128)} async-done(((f32[64,2048]{1,0:T(8,128)}), f32[64,128]{1,0:T(8,128)}) %reduce-scatter.21.cloned.1.call-update) | async-done | bytes 32784 | tf_op jit(solution)/shard_map/reduce_scatter | solution.py:24
  1921.1 74.9 %reduce-scatter.23.cloned.1.call-done = f32[64,128]{1,0:T(8,128)} async-done(((f32[64,2048]{1,0:T(8,128)}), f32[64,128]{1,0:T(8,128)}) %reduce-scatter.23.cloned.1.call-update) | async-done | bytes 32784 | tf_op jit(solution)/shard_map/reduce_scatter | solution.py:67
  1996.8 0.8 fusion.67
  1997.6 426.5 %all-gather.15.cloned.1.call-done = f32[16384,64]{1,0:T(8,128)} async-done(((f32[64,64]{1,0:T(8,128)}), f32[16384,64]{1,0:T(8,128)}) %all-gather.15.cloned.1.call-update) | async-done | bytes 4194320 | tf_op jit(solution)/shard_map/all_gather | solution.py:18
  2424.1 4.0 reduce_sum.39
  2428.2 5.8 cholesky.107
  2435.4 4.9 custom-call.13
  2440.3 0.9 convolution_multiply_fusion
  (64 shorter events, 11.2 us)
Async XLA Ops:
  7.4 24.3 copy-start
  7.4 98.1 %reduce-scatter.25.cloned.1.call-start = ((), (), s32[]{:S(2)}) async-start(), calls=%async_computation.18 | async-start | bytes 1114112
  17.1 3.2 copy-start.1
  23.7 7.9 copy-start.2
  23.7 158.7 %reduce-scatter.27.cloned.1.call-start = ((), (), s32[]{:S(2)}) async-start(), calls=%async_computation.19 | async-start | bytes 1114112
  31.6 474.0 %all-gather.9.cloned.1.call-start = ((), (), s32[]{:S(2)}) async-start(), calls=%async_computation.14 | async-start | bytes 8421376 | tf_op jit(solution)/shard_map/all_gather | solution.py:18
  83.2 559.0 %reduce-scatter.13.cloned.1.call-start = ((), (), s32[]{:S(2)}) async-start(), calls=%async_computation.8 | async-start | bytes 557056 | tf_op jit(solution)/shard_map/reduce_scatter | solution.py:24
  562.2 155.6 %reduce-scatter.15.cloned.1.call-start = ((), (), s32[]{:S(2)}) async-start(), calls=%async_computation.9 | async-start | bytes 557056 | tf_op jit(solution)/shard_map/reduce_scatter | solution.py:67
  605.8 539.3 %all-gather.11.cloned.1.call-start = ((), (), s32[]{:S(2)}) async-start(), calls=%async_computation.15 | async-start | bytes 8421376 | tf_op jit(solution)/shard_map/all_gather | solution.py:18
  719.4 562.2 %reduce-scatter.17.cloned.1.call-start = ((), (), s32[]{:S(2)}) async-start(), calls=%async_computation.10 | async-start | bytes 557056 | tf_op jit(solution)/shard_map/reduce_scatter | solution.py:24
  1201.5 154.8 %reduce-scatter.19.cloned.1.call-start = ((), (), s32[]{:S(2)}) async-start(), calls=%async_computation.11 | async-start | bytes 557056 | tf_op jit(solution)/shard_map/reduce_scatter | solution.py:67
  1245.5 539.1 %all-gather.13.cloned.1.call-start = ((), (), s32[]{:S(2)}) async-start(), calls=%async_computation.16 | async-start | bytes 8421376 | tf_op jit(solution)/shard_map/all_gather | solution.py:18
  1358.0 563.1 %reduce-scatter.21.cloned.1.call-start = ((), (), s32[]{:S(2)}) async-start(), calls=%async_computation.12 | async-start | bytes 557056 | tf_op jit(solution)/shard_map/reduce_scatter | solution.py:24
  1841.0 155.0 %reduce-scatter.23.cloned.1.call-start = ((), (), s32[]{:S(2)}) async-start(), calls=%async_computation.13 | async-start | bytes 557056 | tf_op jit(solution)/shard_map/reduce_scatter | solution.py:67
  1884.7 539.4 %all-gather.15.cloned.1.call-start = ((), (), s32[]{:S(2)}) async-start(), calls=%async_computation.17 | async-start | bytes 8421376 | tf_op jit(solution)/shard_map/all_gather | solution.py:18
Sparse Core Ops, SparseCore 0:
  23.8 81.6 reduce-scatter.24
  108.0 74.4 reduce-scatter.26
  562.4 79.7 reduce-scatter.12
  644.5 73.2 reduce-scatter.14
  1201.6 79.9 reduce-scatter.16
  1284.0 72.3 reduce-scatter.18
  1841.1 79.9 reduce-scatter.20
  1923.6 72.3 reduce-scatter.22
Sparse Core Ops, SparseCore 1:
  83.3 422.3 all-gather.8
  719.5 425.5 all-gather.10
  1358.1 426.5 all-gather.12
  1997.7 426.4 all-gather.14
